TPU v7x, 32 devices: a whole 2x2x4 slice. The times are simulated.
32 devices in a mesh: dp: 16 (over z, y, x), fsdp: 2 (over core).
Axes of the slice: x: 2, y: 2, z: 4, core: 2. Of those that a mesh axis runs over, the one named last changes fastest.
Arguments:
- tokens: bfloat16 [32, 256, 1152], P(('dp', 'fsdp')), may hold values from -6 to 6
- condition: bfloat16 [32, 1152], P(('dp', 'fsdp')), may hold values from -6 to 6
- cotangent: bfloat16 [32, 256, 1152], P(('dp', 'fsdp')), may hold values from -6 to 6
- image_grids: int32 [32, 2], P(('dp', 'fsdp')), may hold values from 12 to 20, as said below
- noise_bins: int32 [32], P(('dp', 'fsdp')), may hold values from 0 to 15, as said below
- bin_weights: int32 [16], replicated, may hold values from 1 to 4
- w_qkv: bfloat16 [1152, 3456], P('dp', 'fsdp'), may hold values from -0.1875 to 0.1875
- b_query: float32 [1152], replicated, may hold values from -3 to 3
- b_value: float32 [1152], replicated, may hold values from -0.625 to 0.625
- w_proj: bfloat16 [1152, 1152], P('dp', 'fsdp'), may hold values from -1.5 to 1.5
- b_proj: float32 [1152], replicated, may hold values from -1.75 to 1.75
- w_fc1: bfloat16 [1152, 4608], P('dp', 'fsdp'), may hold values from -0.1875 to 0.1875
- b_fc1: float32 [4608], replicated, may hold values from -3 to 3
- w_fc2: bfloat16 [4608, 1152], P('dp', 'fsdp'), may hold values from -0.09375 to 0.09375
- b_fc2: float32 [1152], replicated, may hold values from -1.75 to 1.75
- w_ada: bfloat16 [6912, 1152], replicated, may hold values from -0.1875 to 0.1875
- b_ada: float32 [6912], replicated, may hold values from -1.75 to 1.75
Outputs:
- result: bfloat16 [32, 256, 1152], P(('dp', 'fsdp'))
- grad_tokens: bfloat16 [32, 256, 1152], P(('dp', 'fsdp'))
- grad_condition: float32 [32, 1152], P(('dp', 'fsdp'))
- grad_w_qkv: float32 [1152, 3456], P('dp', 'fsdp')
- grad_b_query: float32 [1152], replicated
- grad_b_value: float32 [1152], replicated
- grad_w_proj: float32 [1152, 1152], P('dp', 'fsdp')
- grad_b_proj: float32 [1152], replicated
- grad_w_fc1: float32 [1152, 4608], P('dp', 'fsdp')
- grad_b_fc1: float32 [4608], replicated
- grad_w_fc2: float32 [4608, 1152], P('dp', 'fsdp')
- grad_b_fc2: float32 [1152], replicated
- grad_w_ada: float32 [6912, 1152], P(('dp', 'fsdp'))
- grad_b_ada: float32 [6912], replicated
Inputs may be any that keep to these rules, and one draw needn't show every extreme that they name: `image_grids`: each row is a height and a width that sum to 32; an image's tokens are the first height * width of its 256 slots. `noise_bins`: bin ids never fall along the image slots, and every bin holds at least one image.
All inputs are finite; a program needn't handle non-finite values.
Results may differ from a plain program's by a relative error of at most 0.014.
The roundings to bfloat16 on the way count: a program that leaves them out, or rounds other values in their place, can miss the bound.
Values may be sent and summed in bfloat16 or wider, within the bound.
A program may use at most 256 MiB of HBM per device.

v0:
```python
import jax
import jax.numpy as jnp
from jax import lax
from jax.sharding import PartitionSpec as P

D = 1152
H = 16
HD = 72
BINS = 16
SEQ = 256
NEG_FILL = -1e30
NORM_EPS = 1e-06
GELU_COEF = 0.7978845608028654
CUBIC_COEF = 0.044715
ROWS_DIMS = (((0,), (0,)), ((), ()))
LAST_DIMS = (((1,), (1,)), ((), ()))


def gelu_tanh(values_in):
    return (
        0.5
        * values_in
        * (1.0 + jnp.tanh(GELU_COEF * (values_in + CUBIC_COEF * values_in * values_in * values_in)))
    )


def norm_rows(inputs):
    centered = inputs - jnp.mean(inputs, axis=-1, keepdims=True)
    inverse = lax.rsqrt(jnp.mean(centered * centered, axis=-1, keepdims=True) + NORM_EPS)
    return (centered * inverse, inverse)


def norm_back(grad_normed, normed, inverse):
    centered_grad = grad_normed - jnp.mean(grad_normed, axis=-1, keepdims=True)
    return inverse * (
        centered_grad - normed * jnp.mean(grad_normed * normed, axis=-1, keepdims=True)
    )


def collect_trunk(w_qkv, w_proj, w_fc1, w_fc2):
    paired = (
        lax.all_gather(w_qkv, "fsdp", axis=1, tiled=True),
        lax.all_gather(w_proj, "fsdp", axis=1, tiled=True),
        lax.all_gather(w_fc1, "fsdp", axis=1, tiled=True),
        lax.all_gather(w_fc2, "fsdp", axis=1, tiled=True),
    )
    return (
        lax.all_gather(paired[0], "dp", axis=0, tiled=True),
        lax.all_gather(paired[1], "dp", axis=0, tiled=True),
        lax.all_gather(paired[2], "dp", axis=0, tiled=True),
        lax.all_gather(paired[3], "dp", axis=0, tiled=True),
    )


def masked_scores(query, keys, valid_keys):
    scaled = jnp.einsum(
        "blhc,bmhc->bhlm", query, keys, preferred_element_type=jnp.float32
    ) * HD ** (-0.5)
    return jnp.where(valid_keys[:, None, None, :], scaled, NEG_FILL)


def shards(
    tokens,
    condition,
    cotangent,
    image_grids,
    noise_bins,
    bin_weights,
    w_qkv,
    b_query,
    b_value,
    w_proj,
    b_proj,
    w_fc1,
    b_fc1,
    w_fc2,
    b_fc2,
    w_ada,
    b_ada,
):
    images = tokens.shape[0]
    row_count = images * SEQ
    token_count = image_grids[:, 0] * image_grids[:, 1]
    valid_keys = lax.broadcasted_iota(jnp.int32, (images, SEQ), 1) < token_count[:, None]
    bin_table = (noise_bins[:, None] == lax.broadcasted_iota(jnp.int32, (images, BINS), 1)).astype(
        jnp.float32
    )
    local_counts = jnp.sum(bin_table * token_count[:, None].astype(jnp.float32), axis=0)
    counts = lax.psum(local_counts, ("dp", "fsdp"))
    bin_scale = bin_weights.astype(jnp.float32) * (jnp.sum(counts) / BINS) / counts
    image_scale = jnp.sum(bin_table * bin_scale[None, :], axis=1)
    full_qkv, full_proj, full_fc1, full_fc2 = collect_trunk(w_qkv, w_proj, w_fc1, w_fc2)
    cond_float = condition.astype(jnp.float32)
    silu_cond = jax.nn.silu(cond_float).astype(jnp.bfloat16)
    modul = lax.dot_general(silu_cond, w_ada, LAST_DIMS, preferred_element_type=jnp.float32) + b_ada
    pieces = [modul[:, None, part_index * D : (part_index + 1) * D] for part_index in range(6)]
    shift_one, scale_one, gate_one, shift_two, scale_two, gate_two = pieces
    token_float = tokens.astype(jnp.float32)
    normed_one, inverse_one = norm_rows(token_float)
    attn_in = (
        (normed_one * (1.0 + scale_one) + shift_one).astype(jnp.bfloat16).reshape(row_count, D)
    )
    bias_qkv = jnp.concatenate([b_query, jnp.zeros_like(b_query), b_value])
    qkv_all = (jnp.dot(attn_in, full_qkv, preferred_element_type=jnp.float32) + bias_qkv).astype(
        jnp.bfloat16
    )
    qkv_heads = qkv_all.reshape(images, SEQ, 3, H, HD)
    query, keys, values = (qkv_heads[:, :, 0], qkv_heads[:, :, 1], qkv_heads[:, :, 2])
    scores = masked_scores(query, keys, valid_keys)
    row_max = jnp.max(scores, axis=-1, keepdims=True)
    exponent = jnp.exp(scores - row_max)
    row_total = jnp.sum(exponent, axis=-1, keepdims=True)
    soft_probs = exponent / row_total
    log_total = row_max + jnp.log(row_total)
    attended = jnp.einsum(
        "bhlm,bmhc->blhc",
        soft_probs.astype(jnp.bfloat16),
        values,
        preferred_element_type=jnp.float32,
    )
    attended = attended.astype(jnp.bfloat16).reshape(row_count, D)
    attn_out = (jnp.dot(attended, full_proj, preferred_element_type=jnp.float32) + b_proj).reshape(
        images, SEQ, D
    )
    middle = token_float + gate_one * attn_out
    normed_two, inverse_two = norm_rows(middle)
    mlp_in = (normed_two * (1.0 + scale_two) + shift_two).astype(jnp.bfloat16).reshape(row_count, D)
    hidden = jnp.dot(mlp_in, full_fc1, preferred_element_type=jnp.float32) + b_fc1
    active = gelu_tanh(hidden).astype(jnp.bfloat16)
    branch = (jnp.dot(active, full_fc2, preferred_element_type=jnp.float32) + b_fc2).reshape(
        images, SEQ, D
    )
    result = (middle + gate_two * branch).astype(jnp.bfloat16)
    back_qkv, back_proj, back_fc1, back_fc2 = (full_qkv, full_proj, full_fc1, full_fc2)
    grad_out = (
        cotangent.astype(jnp.float32)
        * (valid_keys.astype(jnp.float32) * image_scale[:, None])[:, :, None]
    )
    d_gate_two = jnp.sum(grad_out * branch, axis=1)
    d_branch = (gate_two * grad_out).astype(jnp.bfloat16).reshape(row_count, D)
    grad_fc2 = lax.dot_general(active, d_branch, ROWS_DIMS, preferred_element_type=jnp.float32)
    bias_fc2 = jnp.sum(d_branch, axis=0, dtype=jnp.float32)
    d_active = lax.dot_general(d_branch, back_fc2, LAST_DIMS, preferred_element_type=jnp.float32)
    gelu_pull = jax.vjp(gelu_tanh, hidden)[1]
    d_hidden = gelu_pull(d_active)[0].astype(jnp.bfloat16)
    grad_fc1 = lax.dot_general(mlp_in, d_hidden, ROWS_DIMS, preferred_element_type=jnp.float32)
    bias_fc1 = jnp.sum(d_hidden, axis=0, dtype=jnp.float32)
    d_mlp_in = lax.dot_general(
        d_hidden, back_fc1, LAST_DIMS, preferred_element_type=jnp.float32
    ).reshape(images, SEQ, D)
    d_shift_two = jnp.sum(d_mlp_in, axis=1)
    d_scale_two = jnp.sum(d_mlp_in * normed_two, axis=1)
    d_middle = grad_out + norm_back(d_mlp_in * (1.0 + scale_two), normed_two, inverse_two)
    d_gate_one = jnp.sum(d_middle * attn_out, axis=1)
    d_attn = (gate_one * d_middle).astype(jnp.bfloat16).reshape(row_count, D)
    grad_proj = lax.dot_general(attended, d_attn, ROWS_DIMS, preferred_element_type=jnp.float32)
    bias_proj = jnp.sum(d_attn, axis=0, dtype=jnp.float32)
    d_attended = lax.dot_general(d_attn, back_proj, LAST_DIMS, preferred_element_type=jnp.float32)
    d_attended = d_attended.astype(jnp.bfloat16).reshape(images, SEQ, H, HD)
    soft_again = jnp.exp(masked_scores(query, keys, valid_keys) - log_total)
    grad_values = jnp.einsum(
        "bhlm,blhc->bmhc",
        soft_again.astype(jnp.bfloat16),
        d_attended,
        preferred_element_type=jnp.float32,
    )
    d_probs = jnp.einsum("blhc,bmhc->bhlm", d_attended, values, preferred_element_type=jnp.float32)
    d_scores = soft_again * (d_probs - jnp.sum(soft_again * d_probs, axis=-1, keepdims=True))
    d_scores = jnp.where(valid_keys[:, None, None, :], d_scores, 0.0).astype(jnp.bfloat16)
    grad_query = jnp.einsum(
        "bhlm,bmhc->blhc", d_scores, keys, preferred_element_type=jnp.float32
    ) * HD ** (-0.5)
    grad_keys = jnp.einsum(
        "bhlm,blhc->bmhc", d_scores, query, preferred_element_type=jnp.float32
    ) * HD ** (-0.5)
    d_qkv = (
        jnp.stack([grad_query, grad_keys, grad_values], axis=2)
        .astype(jnp.bfloat16)
        .reshape(row_count, 3 * D)
    )
    grad_qkv = lax.dot_general(attn_in, d_qkv, ROWS_DIMS, preferred_element_type=jnp.float32)
    bias_query = jnp.sum(d_qkv[:, :D], axis=0, dtype=jnp.float32)
    bias_value = jnp.sum(d_qkv[:, 2 * D :], axis=0, dtype=jnp.float32)
    d_attn_in = lax.dot_general(
        d_qkv, back_qkv, LAST_DIMS, preferred_element_type=jnp.float32
    ).reshape(images, SEQ, D)
    d_shift_one = jnp.sum(d_attn_in, axis=1)
    d_scale_one = jnp.sum(d_attn_in * normed_one, axis=1)
    grad_tokens = (
        d_middle + norm_back(d_attn_in * (1.0 + scale_one), normed_one, inverse_one)
    ).astype(jnp.bfloat16)
    d_modul = jnp.concatenate(
        [d_shift_one, d_scale_one, d_gate_one, d_shift_two, d_scale_two, d_gate_two], axis=1
    ).astype(jnp.bfloat16)
    silu_pull = jax.vjp(jax.nn.silu, cond_float)[1]
    grad_condition = silu_pull(jnp.dot(d_modul, w_ada, preferred_element_type=jnp.float32))[0]
    bias_ada = jnp.sum(d_modul, axis=0, dtype=jnp.float32)
    spread_dp = (
        lax.psum_scatter(grad_qkv, "dp", scatter_dimension=0, tiled=True),
        lax.psum_scatter(grad_proj, "dp", scatter_dimension=0, tiled=True),
        lax.psum_scatter(grad_fc1, "dp", scatter_dimension=0, tiled=True),
        lax.psum_scatter(grad_fc2, "dp", scatter_dimension=0, tiled=True),
    )
    owned = (
        lax.psum_scatter(
            spread_dp[0].astype(jnp.bfloat16), "fsdp", scatter_dimension=1, tiled=True
        ).astype(jnp.float32),
        lax.psum_scatter(
            spread_dp[1].astype(jnp.bfloat16), "fsdp", scatter_dimension=1, tiled=True
        ).astype(jnp.float32),
        lax.psum_scatter(
            spread_dp[2].astype(jnp.bfloat16), "fsdp", scatter_dimension=1, tiled=True
        ).astype(jnp.float32),
        lax.psum_scatter(
            spread_dp[3].astype(jnp.bfloat16), "fsdp", scatter_dimension=1, tiled=True
        ).astype(jnp.float32),
    )
    summed_bias = lax.psum(
        (bias_query, bias_value, bias_proj, bias_fc1, bias_fc2, bias_ada), ("dp", "fsdp")
    )
    share_rows = 6 * D // lax.axis_size(("dp", "fsdp"))
    own_start = lax.axis_index(("dp", "fsdp")) * share_rows
    columns = lax.dynamic_slice_in_dim(
        lax.all_gather(d_modul, ("dp", "fsdp"), axis=0, tiled=True), own_start, share_rows, 1
    )
    grad_ada = lax.dot_general(
        columns,
        lax.all_gather(silu_cond, ("dp", "fsdp"), axis=0, tiled=True),
        ROWS_DIMS,
        preferred_element_type=jnp.float32,
    )
    return (
        result,
        grad_tokens,
        grad_condition,
        owned[0],
        summed_bias[0],
        summed_bias[1],
        owned[1],
        summed_bias[2],
        owned[2],
        summed_bias[3],
        owned[3],
        summed_bias[4],
        grad_ada,
        summed_bias[5],
    )


def solution(mesh):
    in_specs = (
        P(("dp", "fsdp"), None, None),
        P(("dp", "fsdp"), None),
        P(("dp", "fsdp"), None, None),
        P(("dp", "fsdp"), None),
        P(("dp", "fsdp")),
        P(),
        P("dp", "fsdp"),
        P(),
        P(),
        P("dp", "fsdp"),
        P(),
        P("dp", "fsdp"),
        P(),
        P("dp", "fsdp"),
        P(),
        P(),
        P(),
    )
    out_specs = (
        P(("dp", "fsdp"), None, None),
        P(("dp", "fsdp"), None, None),
        P(("dp", "fsdp"), None),
        P("dp", "fsdp"),
        P(),
        P(),
        P("dp", "fsdp"),
        P(),
        P("dp", "fsdp"),
        P(),
        P("dp", "fsdp"),
        P(),
        P(("dp", "fsdp"), None),
        P(),
    )
    return jax.shard_map(shards, mesh=mesh, in_specs=in_specs, out_specs=out_specs, check_vma=False)
```

profile of v0, /device:TPU:0, one launch (start us, length us, event | category | flops | bytes accessed | tf_op | source)
XLA Modules:
  0.0 1598.3 jit_solution(9398244737780951491)
XLA Ops:
  7.2 2.6 all-gather
  24.0 44.7 %psum.49 = f32[16]{0:T(128)S(1)} all-reduce(f32[16]{0:T(128)S(1)} %compare_select_fusion.1), channel_id=1, replica_groups=mesh['dp'=16,'fsdp'=2] {'dp','fsdp'}, use_global_device_ids=true, to_apply=%region_6.7 | all-reduce | flops 16 | bytes 128 | tf_op jit(solution)/shard_map/psum | solution.py:89
  69.3 10.2 convolution_reduce_fusion
  83.8 39.2 %all-gather.10.cloned.1.call-done = bf16[1152,3456]{1,0:T(8,128)(2,1)} async-done(((bf16[72,3456]{1,0:T(8,128)(2,1)}), bf16[1152,3456]{1,0:T(8,128)(2,1)}) %all-gather.10.cloned.1.call-update) | async-done | bytes 7962640 | tf_op jit(solution)/shard_map/all_gather | solution.py:48
  123.0 7.2 fusion.1
  137.6 51.1 %all-gather.12.cloned.1.call-done = bf16[1152,1152]{1,0:T(8,128)(2,1)} async-done(((bf16[72,1152]{1,0:T(8,128)(2,1)}), bf16[1152,1152]{1,0:T(8,128)(2,1)}) %all-gather.12.cloned.1.call-update) | async-done | bytes 2654224 | tf_op jit(solution)/shard_map/all_gather | solution.py:49
  188.7 4.1 fusion.102
  194.2 128.6 %all-gather.14.cloned.1.call-done = bf16[1152,4608]{1,0:T(8,128)(2,1)} async-done(((bf16[72,4608]{1,0:T(8,128)(2,1)}), bf16[1152,4608]{1,0:T(8,128)(2,1)}) %all-gather.14.cloned.1.call-update) | async-done | bytes 10616848 | tf_op jit(solution)/shard_map/all_gather | solution.py:50
  322.8 9.0 convolution_add_fusion
  331.8 125.2 %all-gather.16.cloned.1.call-done = bf16[4608,1152]{1,0:T(8,128)(2,1)} async-done(((bf16[288,1152]{1,0:T(8,128)(2,1)}), bf16[4608,1152]{1,0:T(8,128)(2,1)}) %all-gather.16.cloned.1.call-update) | async-done | bytes 10616848 | tf_op jit(solution)/shard_map/all_gather | solution.py:51
  457.0 10.2 convert_reduce_fusion
  467.2 8.8 fusion.98
  476.1 9.3 fusion.62
  488.5 3.2 fusion.105
  493.4 3.8 convolution_convert_fusion
  499.4 3.8 fusion.73
  503.2 8.6 fusion.43
  511.8 8.6 fusion.49
  520.5 3.2 fusion.37
  524.4 8.1 fusion.86
  533.0 14.1 fusion.89
  547.2 12.1 fusion.95
  560.0 41.9 %all-gather.4 = bf16[32,1,1152]{2,1,0:T(2,128)(2,1)} all-gather(bf16[1,1,1152]{2,1,0:T(2,128)(2,1)S(1)} %copy-done.41), channel_id=1, replica_groups=mesh['dp'=16,'fsdp'=2] {'dp','fsdp'}, dimensions={0}, use_global_device_ids=true | all-gather | bytes 76032 | tf_op jit(solution)/shard_map/all_gather | solution.py:228
  601.9 30.4 %reduce-scatter.33.cloned.1.call-done = f32[72,1152]{1,0:T(8,128)} async-done(((f32[1152,1152]{1,0:T(8,128)}), f32[72,1152]{1,0:T(8,128)}) %reduce-scatter.33.cloned.1.call-update) | async-done | bytes 331792
  634.3 6.7 fusion.60
  642.8 246.3 %reduce-scatter.31.cloned.1.call-done = f32[72,3456]{1,0:T(8,128)} async-done(((f32[1152,3456]{1,0:T(8,128)}), f32[72,3456]{1,0:T(8,128)}) %reduce-scatter.31.cloned.1.call-update) | async-done | bytes 995344
  895.6 3.6 fusion.64
  899.2 307.8 %reduce-scatter.23.cloned.1.call-done = f32[288,1152]{1,0:T(8,128)} async-done(((f32[4608,1152]{1,0:T(8,128)}), f32[288,1152]{1,0:T(8,128)}) %reduce-scatter.23.cloned.1.call-update) | async-done | bytes 1327120 | tf_op jit(solution)/shard_map/reduce_scatter | solution.py:202
  1209.9 47.2 %all-gather.3 = bf16[32,1,6912]{2,1,0:T(2,128)(2,1)S(1)} all-gather(bf16[1,1,6912]{2,1,0:T(2,128)(2,1)S(1)} %bitcast.186), channel_id=1, replica_groups=mesh['dp'=16,'fsdp'=2] {'dp','fsdp'}, dimensions={0}, use_global_device_ids=true | all-gather | bytes 456192 | tf_op jit(solution)/shard_map/all_gather | solution.py:224
  1257.2 271.1 %reduce-scatter.19.cloned.1.call-done = f32[72,4608]{1,0:T(8,128)} async-done(((f32[1152,4608]{1,0:T(8,128)}), f32[72,4608]{1,0:T(8,128)}) %reduce-scatter.19.cloned.1.call-update) | async-done | bytes 1327120 | tf_op jit(solution)/shard_map/reduce_scatter | solution.py:201
  1532.6 41.1 %all-reduce.2 = (f32[1152]{0:T(1024)}, f32[1152]{0:T(1024)}, f32[1152]{0:T(1024)}, f32[4608]{0:T(1024)}, f32[1152]{0:T(1024)}, /*index=5*/f32[6912]{0:T(1024)}) all-reduce(f32[1152]{0:T(1024)S(1)} %get-tuple-element.19, f32[1152]{0:T(1024)S(1)} %get-tuple-element.18, ...), channel_id=1, replica_groups=mesh['dp'=16,'fsdp'=2] {'dp','fsdp'}, use_global_device_ids=true, to_apply=%region_23.24 | all-reduce | flops 16128 | bytes 115200 | tf_op jit(solution)/shard_map/psum | solution.py:218
  1575.2 8.3 fusion.78
  (205 shorter events, 60.5 us)
Async XLA Ops:
  7.2 115.8 %all-gather.10.cloned.1.call-start = ((), (), s32[]{:S(2)}) async-start(), calls=%async_computation.8 | async-start | bytes 8460288 | tf_op jit(solution)/shard_map/all_gather | solution.py:48
  11.5 177.2 %all-gather.12.cloned.1.call-start = ((), (), s32[]{:S(2)}) async-start(), calls=%async_computation.9 | async-start | bytes 2820096 | tf_op jit(solution)/shard_map/all_gather | solution.py:49
  14.5 308.3 %all-gather.14.cloned.1.call-start = ((), (), s32[]{:S(2)}) async-start(), calls=%async_computation.10 | async-start | bytes 11280384 | tf_op jit(solution)/shard_map/all_gather | solution.py:50
  17.0 440.0 %all-gather.16.cloned.1.call-start = ((), (), s32[]{:S(2)}) async-start(), calls=%async_computation.11 | async-start | bytes 11280384 | tf_op jit(solution)/shard_map/all_gather | solution.py:51
  17.1 51.5 %copy-start.22 = (bf16[1,1152]{1,0:T(2,128)(2,1)S(1)}, bf16[1,1152]{1,0:T(2,128)(2,1)}, u32[]{:S(2)}) copy-start(bf16[1,1152]{1,0:T(2,128)(2,1)} %param.18) | copy-start | bytes 6916
  21.3 610.9 %reduce-scatter.33.cloned.1.call-start = ((), (), s32[]{:S(2)}) async-start(), calls=%async_computation.19 | async-start | bytes 5640192
  80.8 52.1 %copy-start.50 = (pred[256]{0:T(512)(128)(4,1)}, pred[256]{0:T(512)(128)(4,1)S(1)}, u32[]{:S(2)}) copy-start(pred[256]{0:T(512)(128)(4,1)S(1)} %iota_compare_fusion) | copy-start | bytes 772
  83.3 39.7 %copy-start.15 = (f32[1152]{0:T(1024)}, f32[1152]{0:T(1024)S(1)}, u32[]{:S(2)}) copy-start(f32[1152]{0:T(1024)S(1)} %get-tuple-element.27) | copy-start | bytes 13828
  83.5 39.5 %copy-start.27 = (f32[256]{0:T(256)}, f32[256]{0:T(256)S(1)}, u32[]{:S(2)}) copy-start(f32[256]{0:T(256)S(1)} %broadcast_multiply_fusion.5) | copy-start | bytes 3076
  491.8 397.3 %reduce-scatter.31.cloned.1.call-start = ((), (), s32[]{:S(2)}) async-start(), calls=%async_computation.18 | async-start | bytes 16920576
  532.5 674.5 %reduce-scatter.23.cloned.1.call-start = ((), (), s32[]{:S(2)}) async-start(), calls=%async_computation.14 | async-start | bytes 22560768 | tf_op jit(solution)/shard_map/reduce_scatter | solution.py:202
  547.1 981.2 %reduce-scatter.19.cloned.1.call-start = ((), (), s32[]{:S(2)}) async-start(), calls=%async_computation.12 | async-start | bytes 22560768 | tf_op jit(solution)/shard_map/reduce_scatter | solution.py:201
  559.3 74.9 %copy-start.29 = (f32[256]{0:T(256)S(1)}, f32[256]{0:T(256)}, u32[]{:S(2)}) copy-start(f32[256]{0:T(256)} %copy-done.27) | copy-start | bytes 3076
  559.3 74.9 %copy-start.38 = (f32[256]{0:T(256)S(1)}, f32[256]{0:T(256)}, u32[]{:S(2)}) copy-start(f32[256]{0:T(256)} %copy-done.36) | copy-start | bytes 3076
  559.3 1024.1 %reduce-scatter.27.cloned.1.call-start = ((), (), s32[]{:S(2)}) async-start(), calls=%async_computation.16 | async-start | bytes 442368
  634.2 951.0 %reduce-scatter.25.cloned.1.call-start = ((), (), s32[]{:S(2)}) async-start(), calls=%async_computation.15 | async-start | bytes 1327104
  642.8 252.8 %copy-start.3 = (f32[256,1152]{1,0:T(8,128)S(1)}, f32[256,1152]{1,0:T(8,128)}, u32[]{:S(2)}) copy-start(f32[256,1152]{1,0:T(8,128)} %get-tuple-element.54) | copy-start | bytes 3538948
  893.4 693.8 %reduce-scatter.29.cloned.1.call-start = ((), (), s32[]{:S(2)}) async-start(), calls=%async_computation.17 | async-start | bytes 1327104
  899.2 310.6 %copy-start.26 = (bf16[1,6912]{1,0:T(2,128)(2,1)S(1)}, bf16[1,6912]{1,0:T(2,128)(2,1)}, u32[]{:S(2)}) copy-start(bf16[1,6912]{1,0:T(2,128)(2,1)} %constant_dynamic-update-slice_fusion.5) | copy-start | bytes 41476
  899.2 310.6 %copy-start.45 = (bf16[1152]{0:T(1024)(128)(2,1)S(1)}, bf16[1152]{0:T(1024)(128)(2,1)}, u32[]{:S(2)}) copy-start(bf16[1152]{0:T(1024)(128)(2,1)} %get-tuple-element.16) | copy-start | bytes 6916
  899.2 310.7 %copy-start.32 = (bf16[1152]{0:T(1024)(128)(2,1)S(1)}, bf16[1152]{0:T(1024)(128)(2,1)}, u32[]{:S(2)}) copy-start(bf16[1152]{0:T(1024)(128)(2,1)} %get-tuple-element.47) | copy-start | bytes 6916
  899.2 310.7 %copy-start.44 = (bf16[1152]{0:T(1024)(128)(2,1)S(1)}, bf16[1152]{0:T(1024)(128)(2,1)}, u32[]{:S(2)}) copy-start(bf16[1152]{0:T(1024)(128)(2,1)} %get-tuple-element.20) | copy-start | bytes 6916
  899.2 310.7 %copy-start.43 = (bf16[1152]{0:T(1024)(128)(2,1)S(1)}, bf16[1152]{0:T(1024)(128)(2,1)}, u32[]{:S(2)}) copy-start(bf16[1152]{0:T(1024)(128)(2,1)} %get-tuple-element.46) | copy-start | bytes 6916
  899.2 310.7 %copy-start.42 = (bf16[1152]{0:T(1024)(128)(2,1)S(1)}, bf16[1152]{0:T(1024)(128)(2,1)}, u32[]{:S(2)}) copy-start(bf16[1152]{0:T(1024)(128)(2,1)} %get-tuple-element.43) | copy-start | bytes 6916
  1209.7 379.6 %reduce-scatter.21.cloned.1.call-start = ((), (), s32[]{:S(2)}) async-start(), calls=%async_computation.13 | async-start | bytes 995328 | tf_op jit(solution)/shard_map/reduce_scatter | solution.py:211
  1257.2 273.8 %copy-start.21 = (bf16[6912]{0:T(1024)(128)(2,1)S(1)}, bf16[6912]{0:T(1024)(128)(2,1)}, u32[]{:S(2)}) copy-start(bf16[6912]{0:T(1024)(128)(2,1)} %custom-call.1) | copy-start | bytes 41476
  1257.2 275.4 %copy-start.33 = (f32[1152]{0:T(1024)S(1)}, f32[1152]{0:T(1024)}, u32[]{:S(2)}) copy-start(f32[1152]{0:T(1024)} %get-tuple-element.38) | copy-start | bytes 13828
  1257.2 275.4 %copy-start.34 = (f32[1152]{0:T(1024)S(1)}, f32[1152]{0:T(1024)}, u32[]{:S(2)}) copy-start(f32[1152]{0:T(1024)} %get-tuple-element.49) | copy-start | bytes 13828
  1257.2 275.4 %copy-start.40 = (f32[4608]{0:T(1024)S(1)}, f32[4608]{0:T(1024)}, u32[]{:S(2)}) copy-start(f32[4608]{0:T(1024)} %get-tuple-element.57) | copy-start | bytes 55300
  1257.2 316.7 %copy-start.12 = (bf16[32,1,1152]{2,1,0:T(2,128)(2,1)S(1)}, bf16[32,1,1152]{2,1,0:T(2,128)(2,1)}, u32[]{:S(2)}) copy-start(bf16[32,1,1152]{2,1,0:T(2,128)(2,1)} %all-gather.4) | copy-start | bytes 221188
  1530.5 44.6 %copy-start.23 = (bf16[1,1152]{1,0:T(2,128)(2,1)S(1)}, bf16[1,1152]{1,0:T(2,128)(2,1)}, u32[]{:S(2)}) copy-start(bf16[1,1152]{1,0:T(2,128)(2,1)} %param.18) | copy-start | bytes 6916
  1530.5 44.6 %copy-start.25 = (f32[1,1152]{1,0:T(1,128)S(1)}, f32[1,1152]{1,0:T(1,128)}, u32[]{:S(2)}) copy-start(f32[1,1152]{1,0:T(1,128)} %copy-done.24) | copy-start | bytes 13828
  (33 other events, 235.5 us)
Sparse Core Ops, SparseCore 0:
  11.6 111.3 all-gather.9
  126.2 62.4 all-gather.11
  191.5 131.2 all-gather.13
  326.0 130.9 all-gather.15
  491.9 140.3 reduce-scatter.32
  637.9 251.1 reduce-scatter.30
  895.1 311.8 reduce-scatter.22
  1213.0 315.2 reduce-scatter.18
  1531.1 6.8 reduce-scatter.26
  1540.2 9.3 reduce-scatter.24
  1551.8 9.3 reduce-scatter.28
  1564.0 9.2 reduce-scatter.20
where the time goes:
time: 1600 us
  waiting for transfers between devices  1200 us (75%)
  blocking collectives  184 us (12%)
  matrix products  143 us (9%)
  other arithmetic  26.5 us (2%)
  local copies, waits for them, and re-layouts  25.3 us (2%)
  between operations  17.6 us (1%)
    reduce_scatter x1, waiting for transfers between devices, shards(): lax.psum_scatter(grad_fc2, 'dp', scatter_dimension=0, tiled=True)  308 us
    unnamed x17, waiting for transfers between devices  277 us
    reduce_scatter x1, waiting for transfers between devices, shards(): lax.psum_scatter(grad_fc1, 'dp', scatter_dimension=0, tiled=True)  271 us
    all_gather x1, waiting for transfers between devices, collect_trunk(): lax.all_gather(paired[2], 'dp', axis=0, tiled=True)  129 us
    all_gather x1, waiting for transfers between devices, collect_trunk(): lax.all_gather(paired[3], 'dp', axis=0, tiled=True)  125 us
    all_gather x1, waiting for transfers between devices, collect_trunk(): lax.all_gather(paired[1], 'dp', axis=0, tiled=True)  51.1 us
    all_gather x1, blocking collectives, shards(): lax.all_gather(d_modul, ('dp', 'fsdp'), axis=0, tiled=True)  47.2 us
    psum x1, blocking collectives, shards(): counts = lax.psum(local_counts, ('dp', 'fsdp'))  44.7 us
  transfers between devices with their start and end apart: 12, of which 8 were waited for; matrix products, arithmetic and copies ran while one was open for 10% of the time, Pallas kernels for 0%

commit v1 on v0

--- a/solution.py
+++ b/solution.py
@@ -16,6 +16,18 @@
 LAST_DIMS = (((1,), (1,)), ((), ()))
 
 
+def doubled_up(x, axis, dim):
+    ways, here, step = (lax.axis_size(axis), lax.axis_index(axis), x.shape[dim])
+    line, have = (x, 1)
+    while have < ways:
+        line = jnp.concatenate(
+            [line, lax.ppermute(line, axis, [(d, (d - have) % ways) for d in range(ways)])],
+            axis=dim,
+        )
+        have = 2 * have
+    return jnp.roll(line, here * step, axis=dim)
+
+
 def gelu_tanh(values_in):
     return (
         0.5
@@ -45,7 +57,7 @@
         lax.all_gather(w_fc2, "fsdp", axis=1, tiled=True),
     )
     return (
-        lax.all_gather(paired[0], "dp", axis=0, tiled=True),
+        doubled_up(paired[0], "dp", 0),
         lax.all_gather(paired[1], "dp", axis=0, tiled=True),
         lax.all_gather(paired[2], "dp", axis=0, tiled=True),
         lax.all_gather(paired[3], "dp", axis=0, tiled=True),

time: 1600 us -> 1710 us (1.069)
  blocking collectives: 184 us -> 358 us
  waiting for transfers between devices: 1200 us -> 1110 us
    psum x1, blocking collectives: 44.7 us -> 215 us  [shards(): counts = lax.psum(local_counts, ('dp', 'fsdp'))]
    ppermute x0 -> x4, waiting for transfers between devices: none -> 80.9 us  [doubled_up(): lax.ppermute(line, axis, [(d, (d - have) % ways) for d in range(ways)])]
    all_gather x1, waiting for transfers between devices: 129 us -> 51.8 us  [collect_trunk(): lax.all_gather(paired[2], 'dp', axis=0, tiled=True)]
    all_gather x1, waiting for transfers between devices: 51.1 us -> 0.01 us  [collect_trunk(): lax.all_gather(paired[1], 'dp', axis=0, tiled=True)]
    all_gather x1 -> x0, waiting for transfers between devices: 39.2 us -> none  [collect_trunk(): lax.all_gather(paired[0], 'dp', axis=0, tiled=True)]
    unnamed x17 -> x16, waiting for transfers between devices: 277 us -> 275 us
  transfers between devices with their start and end apart: 12 -> 15, of which waited for: 8 -> 9; matrix products, arithmetic and copies ran while one was open for 10% -> 9% of each run, Pallas kernels for 0% -> 0%
where the time goes in v1:
time: 1710 us
  waiting for transfers between devices  1110 us (65%)
  blocking collectives  358 us (21%)
  matrix products  140 us (8%)
  local copies, waits for them, and re-layouts  38.4 us (2%)
  other arithmetic  29.5 us (2%)
  between operations  17.5 us (1%)
    reduce_scatter x1, waiting for transfers between devices, shards(): lax.psum_scatter(grad_fc2, 'dp', scatter_dimension=0, tiled=True)  308 us
    unnamed x16, waiting for transfers between devices  275 us
    reduce_scatter x1, waiting for transfers between devices, shards(): lax.psum_scatter(grad_fc1, 'dp', scatter_dimension=0, tiled=True)  272 us
    psum x1, blocking collectives, shards(): counts = lax.psum(local_counts, ('dp', 'fsdp'))  215 us
    all_gather x1, waiting for transfers between devices, collect_trunk(): lax.all_gather(paired[3], 'dp', axis=0, tiled=True)  125 us
    ppermute x4, waiting for transfers between devices, doubled_up(): lax.ppermute(line, axis, [(d, (d - have) % ways) for d in range(ways)])  80.9 us
    all_gather x1, waiting for transfers between devices, collect_trunk(): lax.all_gather(paired[2], 'dp', axis=0, tiled=True)  51.8 us
    all_gather x1, blocking collectives, shards(): lax.all_gather(d_modul, ('dp', 'fsdp'), axis=0, tiled=True)  47.2 us
  transfers between devices with their start and end apart: 15, of which 9 were waited for; matrix products, arithmetic and copies ran while one was open for 9% of the time, Pallas kernels for 0%

profile of v1, /device:TPU:0, one launch (start us, length us, event | category | flops | bytes accessed | tf_op | source)
XLA Modules:
  0.0 1705.1 jit_solution(14160008996555376213)
XLA Ops:
  10.7 5.0 all_gather.30
  23.2 6.7 collective-permute-start
  29.9 14.8 collective-permute-done
  44.8 25.6 %collective-permute-done.1 = bf16[144,3456]{1,0:T(8,128)(2,1)S(1)} collective-permute-done((bf16[144,3456]{1,0:T(8,128)(2,1)S(1)}, bf16[144,3456]{1,0:T(8,128)(2,1)S(1)}, u32[]{:S(2)}, u32[]{:S(2)}) %collective-permute-start.1) | collective-permute-done | bytes 995360 | tf_op jit(solution)/shard_map/ppermute | solution.py:24
  75.0 40.5 %collective-permute-done.2 = bf16[288,3456]{1,0:T(8,128)(2,1)S(1)} collective-permute-done((bf16[288,3456]{1,0:T(8,128)(2,1)S(1)}, bf16[288,3456]{1,0:T(8,128)(2,1)S(1)}, u32[]{:S(2)}, u32[]{:S(2)}) %collective-permute-start.2) | collective-permute-done | bytes 1990688 | tf_op jit(solution)/shard_map/ppermute | solution.py:24
  118.4 10.2 convolution_reduce_fusion
  128.6 215.0 %psum.49 = f32[16]{0:T(128)S(1)} all-reduce(f32[16]{0:T(128)S(1)} %compare_select_fusion.1), channel_id=1, replica_groups=mesh['dp'=16,'fsdp'=2] {'dp','fsdp'}, use_global_device_ids=true, to_apply=%region_6.7 | all-reduce | flops 16 | bytes 128 | tf_op jit(solution)/shard_map/psum | solution.py:101
  355.0 5.4 copy-done.55
  360.4 4.1 fusion.8
  372.1 4.0 fusion.113
  377.5 51.8 %all-gather.11.cloned.1.call-done = bf16[1152,4608]{1,0:T(8,128)(2,1)} async-done(((bf16[72,4608]{1,0:T(8,128)(2,1)}), bf16[1152,4608]{1,0:T(8,128)(2,1)}) %all-gather.11.cloned.1.call-update) | async-done | bytes 10616848 | tf_op jit(solution)/shard_map/all_gather | solution.py:62
  429.3 9.0 convolution_add_fusion
  438.3 125.3 %all-gather.13.cloned.1.call-done = bf16[4608,1152]{1,0:T(8,128)(2,1)} async-done(((bf16[288,1152]{1,0:T(8,128)(2,1)}), bf16[4608,1152]{1,0:T(8,128)(2,1)}) %all-gather.13.cloned.1.call-update) | async-done | bytes 10616848 | tf_op jit(solution)/shard_map/all_gather | solution.py:63
  563.6 10.2 convert_reduce_fusion
  573.9 8.8 fusion.109
  582.8 9.3 fusion.71
  600.3 3.8 convolution_convert_fusion
  606.2 3.7 fusion.82
  609.9 8.5 fusion.52
  618.4 8.6 fusion.58
  631.8 8.2 fusion.97
  641.0 14.1 fusion.100
  655.8 12.0 fusion.106
  668.4 42.1 %all-gather.4 = bf16[32,1,1152]{2,1,0:T(2,128)(2,1)} all-gather(bf16[1,1,1152]{2,1,0:T(2,128)(2,1)S(1)} %copy-done.50), channel_id=1, replica_groups=mesh['dp'=16,'fsdp'=2] {'dp','fsdp'}, dimensions={0}, use_global_device_ids=true | all-gather | bytes 76032 | tf_op jit(solution)/shard_map/all_gather | solution.py:240
  710.5 28.6 %reduce-scatter.33.cloned.1.call-done = f32[72,1152]{1,0:T(8,128)} async-done(((f32[1152,1152]{1,0:T(8,128)}), f32[72,1152]{1,0:T(8,128)}) %reduce-scatter.33.cloned.1.call-update) | async-done | bytes 331792
  741.1 6.7 fusion.69
  749.6 246.3 %reduce-scatter.31.cloned.1.call-done = f32[72,3456]{1,0:T(8,128)} async-done(((f32[1152,3456]{1,0:T(8,128)}), f32[72,3456]{1,0:T(8,128)}) %reduce-scatter.31.cloned.1.call-update) | async-done | bytes 995344
  1006.1 307.7 %reduce-scatter.23.cloned.1.call-done = f32[288,1152]{1,0:T(8,128)} async-done(((f32[4608,1152]{1,0:T(8,128)}), f32[288,1152]{1,0:T(8,128)}) %reduce-scatter.23.cloned.1.call-update) | async-done | bytes 1327120 | tf_op jit(solution)/shard_map/reduce_scatter | solution.py:214
  1316.7 47.2 %all-gather.3 = bf16[32,1,6912]{2,1,0:T(2,128)(2,1)S(1)} all-gather(bf16[1,1,6912]{2,1,0:T(2,128)(2,1)S(1)} %bitcast.189), channel_id=1, replica_groups=mesh['dp'=16,'fsdp'=2] {'dp','fsdp'}, dimensions={0}, use_global_device_ids=true | all-gather | bytes 456192 | tf_op jit(solution)/shard_map/all_gather | solution.py:236
  1363.9 271.6 %reduce-scatter.19.cloned.1.call-done = f32[72,4608]{1,0:T(8,128)} async-done(((f32[1152,4608]{1,0:T(8,128)}), f32[72,4608]{1,0:T(8,128)}) %reduce-scatter.19.cloned.1.call-update) | async-done | bytes 1327120 | tf_op jit(solution)/shard_map/reduce_scatter | solution.py:213
  1639.8 41.1 %all-reduce.2 = (f32[1152]{0:T(1024)}, f32[1152]{0:T(1024)}, f32[1152]{0:T(1024)}, f32[4608]{0:T(1024)}, f32[1152]{0:T(1024)}, /*index=5*/f32[6912]{0:T(1024)}) all-reduce(f32[1152]{0:T(1024)S(1)} %get-tuple-element.19, f32[1152]{0:T(1024)S(1)} %get-tuple-element.18, ...), channel_id=1, replica_groups=mesh['dp'=16,'fsdp'=2] {'dp','fsdp'}, use_global_device_ids=true, to_apply=%region_23.24 | all-reduce | flops 16128 | bytes 115200 | tf_op jit(solution)/shard_map/psum | solution.py:230
  1682.3 8.3 fusion.87
  (245 shorter events, 83.5 us)
Async XLA Ops:
  7.2 364.9 %all-gather.9.cloned.1.call-start = ((), (), s32[]{:S(2)}) async-start(), calls=%async_computation.8 | async-start | bytes 2820096 | tf_op jit(solution)/shard_map/all_gather | solution.py:61
  10.6 418.7 %all-gather.11.cloned.1.call-start = ((), (), s32[]{:S(2)}) async-start(), calls=%async_computation.9 | async-start | bytes 11280384 | tf_op jit(solution)/shard_map/all_gather | solution.py:62
  15.8 547.9 %all-gather.13.cloned.1.call-start = ((), (), s32[]{:S(2)}) async-start(), calls=%async_computation.10 | async-start | bytes 11280384 | tf_op jit(solution)/shard_map/all_gather | solution.py:63
  20.2 718.9 %reduce-scatter.33.cloned.1.call-start = ((), (), s32[]{:S(2)}) async-start(), calls=%async_computation.18 | async-start | bytes 5640192
  23.2 21.4 %collective-permute-start = (bf16[72,3456]{1,0:T(8,128)(2,1)S(1)}, bf16[72,3456]{1,0:T(8,128)(2,1)S(1)}, u32[]{:S(2)}, u32[]{:S(2)}) collective-permute-start(bf16[72,3456]{1,0:T(8,128)(2,1)S(1)} %bitcast.162), channel_id=1, source_target_pairs={{0,30},{2,0},{4,2},{6,4},{8,6},{10,8},{12,10},{14,12},{16,14},{18,... | collective-permute-start | bytes 1493000 | tf_op jit(solution)/shard_map/ppermute | solution.py:24
  44.8 25.6 %collective-permute-start.1 = (bf16[144,3456]{1,0:T(8,128)(2,1)S(1)}, bf16[144,3456]{1,0:T(8,128)(2,1)S(1)}, u32[]{:S(2)}, u32[]{:S(2)}) collective-permute-start(bf16[144,3456]{1,0:T(8,128)(2,1)S(1)} %pad_maximum_fusion.2), channel_id=1, source_target_pairs={{0,28},{2,30},{4,0},{6,2},{8,4},{10,6},{12,8},{14,10},{16,12},{18,... | collective-permute-start | bytes 2985992 | tf_op jit(solution)/shard_map/ppermute | solution.py:24
  70.5 45.0 %collective-permute-start.2 = (bf16[288,3456]{1,0:T(8,128)(2,1)S(1)}, bf16[288,3456]{1,0:T(8,128)(2,1)S(1)}, u32[]{:S(2)}, u32[]{:S(2)}) collective-permute-start(bf16[288,3456]{1,0:T(8,128)(2,1)S(1)} %pad_maximum_fusion.1), channel_id=1, source_target_pairs={{0,24},{2,26},{4,28},{6,30},{8,0},{10,2},{12,4},{14,6},{16,8},{18,... | collective-permute-start | bytes 5971976 | tf_op jit(solution)/shard_map/ppermute | solution.py:24
  117.7 231.4 %collective-permute-start.3 = (bf16[576,3456]{1,0:T(8,128)(2,1)}, bf16[576,3456]{1,0:T(8,128)(2,1)}, u32[]{:S(2)}, u32[]{:S(2)}) collective-permute-start(bf16[576,3456]{1,0:T(8,128)(2,1)} %pad_maximum_fusion), channel_id=1, source_target_pairs={{0,16},{2,18},{4,20},{6,22},{8,24},{10,26},{12,28},{14,30},{16,0},... | collective-permute-start | bytes 11943944 | tf_op jit(solution)/shard_map/ppermute | solution.py:24
  118.4 229.0 %copy-start.58 = (f32[1152]{0:T(1024)S(1)}, f32[1152]{0:T(1024)}, u32[]{:S(2)}) copy-start(f32[1152]{0:T(1024)} %param.25) | copy-start | bytes 13828
  118.4 229.6 %copy-start.1 = (bf16[1,256,1152]{2,1,0:T(8,128)(2,1)S(1)}, bf16[1,256,1152]{2,1,0:T(8,128)(2,1)}, u32[]{:S(2)}) copy-start(bf16[1,256,1152]{2,1,0:T(8,128)(2,1)} %param.17) | copy-start | bytes 1769476
  598.4 397.4 %reduce-scatter.31.cloned.1.call-start = ((), (), s32[]{:S(2)}) async-start(), calls=%async_computation.17 | async-start | bytes 16920576
  639.9 673.8 %reduce-scatter.23.cloned.1.call-start = ((), (), s32[]{:S(2)}) async-start(), calls=%async_computation.13 | async-start | bytes 22560768 | tf_op jit(solution)/shard_map/reduce_scatter | solution.py:214
  655.1 980.4 %reduce-scatter.19.cloned.1.call-start = ((), (), s32[]{:S(2)}) async-start(), calls=%async_computation.11 | async-start | bytes 22560768 | tf_op jit(solution)/shard_map/reduce_scatter | solution.py:213
  667.8 1022.8 %reduce-scatter.27.cloned.1.call-start = ((), (), s32[]{:S(2)}) async-start(), calls=%async_computation.15 | async-start | bytes 442368
  741.0 951.3 %reduce-scatter.25.cloned.1.call-start = ((), (), s32[]{:S(2)}) async-start(), calls=%async_computation.14 | async-start | bytes 1327104
  747.8 254.7 %copy-start.9 = (f32[256,1152]{1,0:T(8,128)S(1)}, f32[256,1152]{1,0:T(8,128)}, u32[]{:S(2)}) copy-start(f32[256,1152]{1,0:T(8,128)} %get-tuple-element.54) | copy-start | bytes 3538948
  747.8 254.7 %copy-start.37 = (f32[256]{0:T(256)S(1)}, f32[256]{0:T(256)}, u32[]{:S(2)}) copy-start(f32[256]{0:T(256)} %copy-done.35) | copy-start | bytes 3076
  1000.2 694.1 %reduce-scatter.29.cloned.1.call-start = ((), (), s32[]{:S(2)}) async-start(), calls=%async_computation.16 | async-start | bytes 1327104
  1006.1 310.5 %copy-start.34 = (bf16[1,6912]{1,0:T(2,128)(2,1)S(1)}, bf16[1,6912]{1,0:T(2,128)(2,1)}, u32[]{:S(2)}) copy-start(bf16[1,6912]{1,0:T(2,128)(2,1)} %constant_dynamic-update-slice_fusion.15) | copy-start | bytes 41476
  1006.1 310.5 %copy-start.54 = (bf16[1152]{0:T(1024)(128)(2,1)S(1)}, bf16[1152]{0:T(1024)(128)(2,1)}, u32[]{:S(2)}) copy-start(bf16[1152]{0:T(1024)(128)(2,1)} %get-tuple-element.16) | copy-start | bytes 6916
  1006.1 310.5 %copy-start.41 = (bf16[1152]{0:T(1024)(128)(2,1)S(1)}, bf16[1152]{0:T(1024)(128)(2,1)}, u32[]{:S(2)}) copy-start(bf16[1152]{0:T(1024)(128)(2,1)} %get-tuple-element.47) | copy-start | bytes 6916
  1006.1 310.5 %copy-start.53 = (bf16[1152]{0:T(1024)(128)(2,1)S(1)}, bf16[1152]{0:T(1024)(128)(2,1)}, u32[]{:S(2)}) copy-start(bf16[1152]{0:T(1024)(128)(2,1)} %get-tuple-element.20) | copy-start | bytes 6916
  1006.1 310.6 %copy-start.52 = (bf16[1152]{0:T(1024)(128)(2,1)S(1)}, bf16[1152]{0:T(1024)(128)(2,1)}, u32[]{:S(2)}) copy-start(bf16[1152]{0:T(1024)(128)(2,1)} %get-tuple-element.46) | copy-start | bytes 6916
  1006.1 310.6 %copy-start.51 = (bf16[1152]{0:T(1024)(128)(2,1)S(1)}, bf16[1152]{0:T(1024)(128)(2,1)}, u32[]{:S(2)}) copy-start(bf16[1152]{0:T(1024)(128)(2,1)} %get-tuple-element.43) | copy-start | bytes 6916
  1316.4 321.7 %copy-start.29 = (bf16[6912]{0:T(1024)(128)(2,1)S(1)}, bf16[6912]{0:T(1024)(128)(2,1)}, u32[]{:S(2)}) copy-start(bf16[6912]{0:T(1024)(128)(2,1)} %custom-call.1) | copy-start | bytes 41476
  1316.4 323.3 %copy-start.42 = (f32[1152]{0:T(1024)S(1)}, f32[1152]{0:T(1024)}, u32[]{:S(2)}) copy-start(f32[1152]{0:T(1024)} %get-tuple-element.38) | copy-start | bytes 13828
  1316.5 323.3 %copy-start.43 = (f32[1152]{0:T(1024)S(1)}, f32[1152]{0:T(1024)}, u32[]{:S(2)}) copy-start(f32[1152]{0:T(1024)} %get-tuple-element.49) | copy-start | bytes 13828
  1316.5 323.3 %copy-start.49 = (f32[4608]{0:T(1024)S(1)}, f32[4608]{0:T(1024)}, u32[]{:S(2)}) copy-start(f32[4608]{0:T(1024)} %get-tuple-element.57) | copy-start | bytes 55300
  1316.5 364.5 %copy-start.19 = (bf16[32,1,1152]{2,1,0:T(2,128)(2,1)S(1)}, bf16[32,1,1152]{2,1,0:T(2,128)(2,1)}, u32[]{:S(2)}) copy-start(bf16[32,1,1152]{2,1,0:T(2,128)(2,1)} %all-gather.4) | copy-start | bytes 221188
  1316.5 380.0 %reduce-scatter.21.cloned.1.call-start = ((), (), s32[]{:S(2)}) async-start(), calls=%async_computation.12 | async-start | bytes 995328 | tf_op jit(solution)/shard_map/reduce_scatter | solution.py:223
  1363.9 318.4 %copy-start.31 = (bf16[1,1152]{1,0:T(2,128)(2,1)S(1)}, bf16[1,1152]{1,0:T(2,128)(2,1)}, u32[]{:S(2)}) copy-start(bf16[1,1152]{1,0:T(2,128)(2,1)} %param.18) | copy-start | bytes 6916
  1363.9 318.4 %copy-start.33 = (f32[1,1152]{1,0:T(1,128)S(1)}, f32[1,1152]{1,0:T(1,128)}, u32[]{:S(2)}) copy-start(f32[1,1152]{1,0:T(1,128)} %copy-done.32) | copy-start | bytes 13828
  (47 other events, 1176.0 us)
Sparse Core Ops, SparseCore 0:
  11.3 216.8 all-gather.8
  231.0 198.2 all-gather.10
  432.7 130.9 all-gather.12
  598.6 140.4 reduce-scatter.32
  744.7 251.0 reduce-scatter.30
  1001.7 312.0 reduce-scatter.22
  1319.8 315.6 reduce-scatter.18
  1638.3 6.8 reduce-scatter.26
  1647.5 9.3 reduce-scatter.24
  1659.0 9.3 reduce-scatter.28
  1671.2 9.2 reduce-scatter.20
